TPU v7x, 512 devices: a whole 4x4x16 slice. The times are simulated.
512 devices in a mesh: blk: 32 (over x, z_lo), rep: 16 (over z_hi, y, core).
Axes of the slice: x: 4, y: 4, z: 16 (z_hi: 2, z_lo: 8; z = z_hi * 8 + z_lo), core: 2. Of those that a mesh axis runs over, the one named last changes fastest.
Arguments:
- signals: bfloat16 [32768, 8192], P('rep', 'blk'), may hold values from -6 to 6
- omega: float32 [32, 5, 256, 256], P('blk', None, 'rep'), may hold values from -1.2 to 3, as said below
- pattern: int32 [32, 5], P('blk'), may hold values from 0 to 31, as said below
Outputs:
- omega_next: float32 [32, 5, 256, 256], P('blk', None, 'rep')
Inputs may be any that keep to these rules, and one draw needn't show every extreme that they name: pattern[i, 0] = i. For two distinct whole numbers A and B from 1 to 15, the same in every row, pattern[i, 1] to pattern[i, 4] are i + A, i - A, i + B and i - B modulo 32 in some order, the same order in every row. Omega is symmetric: omega[i, k] is the transpose of omega[pattern[i, k], k2] where pattern[pattern[i, k], k2] = i. The diagonal entries of omega[i, 0] lie between 1 and 3.
All inputs are finite; a program needn't handle non-finite values.
Results may differ from a plain program's by a relative error of at most 0.0033.
Values may be sent and summed in bfloat16 or wider, within the bound.
A program may use at most 128 MiB of HBM per device.

v0:
```python
import jax
import jax.numpy as jnp
from jax import lax
from jax.sharding import PartitionSpec as P

STEP_SIZE = 0.5
PENALTY = 0.1


def shifted_2(block, axis, distance):
    devices = range(lax.axis_size(axis))
    route = [((i - distance) % len(devices), i) for i in devices]
    return lax.ppermute(block, axis, route)


def advance(stacked, shifted, distance, section_index):
    chosen = jnp.mod(distance // (1 << section_index), 2) == 1
    return jnp.where(chosen[:, None, None], shifted, stacked)


def slot_order(drawn_offsets, team_count):
    slot_ids = jnp.arange(drawn_offsets.shape[0], dtype=jnp.int32)
    partner = jnp.argmax(drawn_offsets == team_count - drawn_offsets[1])
    third = jnp.where(partner == 2, 3, 2).astype(jnp.int32)
    fourth = jnp.where(partner == 4, 3, 4).astype(jnp.int32)
    order = jnp.stack([jnp.zeros((), jnp.int32), jnp.ones((), jnp.int32), partner, third, fourth])
    inverse = jnp.argmax(order[None, :] == slot_ids[:, None], axis=1)
    return (order, inverse)


def per_device(signals, omega, pattern):
    team_count = lax.axis_size("blk")
    replica_count = lax.axis_size("rep")
    level_count = team_count.bit_length() - 1
    team_index = lax.axis_index("blk")
    replica_index = lax.axis_index("rep")
    slot_count = omega.shape[1]
    tile_rows = omega.shape[2]
    tile_width = omega.shape[3]
    time_length = signals.shape[0] * replica_count
    drawn_offsets = jnp.mod(pattern[0] - team_index, team_count)
    order, inverse = slot_order(drawn_offsets, team_count)
    offsets = drawn_offsets[order]
    own_tiles = omega[0][order]
    panels = lax.all_gather(omega.astype(jnp.bfloat16), "rep", axis=2, tiled=True)[0][order]
    remote = jnp.broadcast_to(signals[None], (slot_count - 1,) + signals.shape)
    distance = offsets[1:]
    for section_index in range(level_count):
        shifted = shifted_2(remote, "blk", -(1 << section_index))
        remote = advance(remote, shifted, distance, section_index)
    gathered = jnp.concatenate([signals[None], remote], axis=0)
    mixed = jnp.einsum("ktc,kdc->td", gathered, panels, preferred_element_type=jnp.float32).astype(
        jnp.bfloat16
    )
    left_terms = jnp.einsum("td,ktc->kdc", mixed, gathered, preferred_element_type=jnp.float32)
    stacked = jnp.concatenate([left_terms, jnp.swapaxes(left_terms, 1, 2)], axis=0)
    first_row = replica_index * tile_rows
    summed = lax.psum(stacked, "rep")
    summed = lax.dynamic_slice_in_dim(summed, first_row, tile_rows, 1)
    own_terms = summed[:slot_count]
    flipped = summed[slot_count:]
    mirrored = [
        flipped[slot_index + 1] if slot_index % 2 == 1 else flipped[slot_index - 1]
        for slot_index in range(1, slot_count)
    ]
    outgoing = jnp.stack(mirrored)
    distance = offsets[1:]
    for section_index in range(level_count):
        shifted = shifted_2(outgoing, "blk", -(1 << section_index))
        outgoing = advance(outgoing, shifted, distance, section_index)
    returned = jnp.concatenate([flipped[0:1], outgoing], axis=0)
    gradient = (own_terms + returned) / (2.0 * time_length)
    column_ids = jnp.arange(tile_width, dtype=jnp.int32)
    row_ids = first_row + jnp.arange(tile_rows, dtype=jnp.int32)
    diagonal_mask = column_ids[None, :] == row_ids[:, None]
    diag_values = jnp.sum(jnp.where(diagonal_mask, own_tiles[0], 0.0), axis=1)
    first_grad = gradient[0] - jnp.where(diagonal_mask, (1.0 / diag_values)[:, None], 0.0)
    gradient = jnp.concatenate([first_grad[None], gradient[1:]], axis=0)
    updated = own_tiles - STEP_SIZE * gradient
    shrunk = jnp.sign(updated) * jnp.maximum(jnp.abs(updated) - STEP_SIZE * PENALTY, 0.0)
    slot_ids = jnp.arange(slot_count, dtype=jnp.int32)
    keep_mask = (slot_ids[:, None, None] == 0) & diagonal_mask[None]
    result = jnp.where(keep_mask, updated, shrunk)
    return result[inverse][None]


def solution(mesh):
    return jax.shard_map(
        per_device,
        mesh=mesh,
        in_specs=(P("rep", "blk"), P("blk", None, "rep", None), P("blk", None)),
        out_specs=P("blk", None, "rep", None),
        check_vma=False,
    )
```

profile of v0, /device:TPU:230, one launch (start us, length us, event | category | flops | bytes accessed | tf_op | source)
XLA Modules:
  0.0 1216.6 jit_solution(44980131006456918)
XLA Ops:
  6.5 3.5 broadcast_in_dim.114
  10.1 2.0 collective-permute-start
  16.6 96.7 %collective-permute-done = bf16[4,2048,256]{2,1,0:T(8,128)(2,1)} collective-permute-done((bf16[4,2048,256]{2,1,0:T(8,128)(2,1)}, bf16[4,2048,256]{2,1,0:T(8,128)(2,1)}, u32[]{:S(2)}, u32[]{:S(2)}) %collective-permute-start) | collective-permute-done | bytes 4194336 | tf_op jit(solution)/shard_map/ppermute | solution.py:13
  113.3 2.8 broadcast_select_fusion
  116.1 1.9 collective-permute-start.1
  118.0 180.3 %collective-permute-done.1 = bf16[4,2048,256]{2,1,0:T(8,128)(2,1)S(1)} collective-permute-done((bf16[4,2048,256]{2,1,0:T(8,128)(2,1)S(1)}, bf16[4,2048,256]{2,1,0:T(8,128)(2,1)S(1)}, u32[]{:S(2)}, u32[]{:S(2)}) %collective-permute-start.1) | collective-permute-done | bytes 4194336 | tf_op jit(solution)/shard_map/ppermute | solution.py:13
  298.3 2.8 broadcast_select_fusion.1
  301.1 1.9 collective-permute-start.2
  303.0 356.7 %collective-permute-done.2 = bf16[4,2048,256]{2,1,0:T(8,128)(2,1)S(1)} collective-permute-done((bf16[4,2048,256]{2,1,0:T(8,128)(2,1)S(1)}, bf16[4,2048,256]{2,1,0:T(8,128)(2,1)S(1)}, u32[]{:S(2)}, u32[]{:S(2)}) %collective-permute-start.2) | collective-permute-done | bytes 4194336 | tf_op jit(solution)/shard_map/ppermute | solution.py:13
  660.3 1.9 collective-permute-start.3
  662.2 93.7 %collective-permute-done.3 = bf16[4,2048,256]{2,1,0:T(8,128)(2,1)S(1)} collective-permute-done((bf16[4,2048,256]{2,1,0:T(8,128)(2,1)S(1)}, bf16[4,2048,256]{2,1,0:T(8,128)(2,1)S(1)}, u32[]{:S(2)}, u32[]{:S(2)}) %collective-permute-start.3) | collective-permute-done | bytes 4194336 | tf_op jit(solution)/shard_map/ppermute | solution.py:13
  755.9 2.4 broadcast_select_fusion.3
  760.2 45.1 %all_gather.3 = bf16[1,5,256,256]{3,2,1,0:T(8,128)(2,1)S(1)} all-gather(bf16[1,5,16,256]{3,2,1,0:T(8,128)(2,1)S(1)} %convert_element_type.6), channel_id=1, replica_groups=mesh['blk'=32,'rep'=16] {'rep'}, dimensions={2}, use_global_device_ids=true | all-gather | bytes 696320 | tf_op jit(solution)/shard_map/all_gather | solution.py:45
  805.9 47.7 %collective-permute-done.4 = bf16[4,2048,256]{2,1,0:T(8,128)(2,1)} collective-permute-done((bf16[4,2048,256]{2,1,0:T(8,128)(2,1)}, bf16[4,2048,256]{2,1,0:T(8,128)(2,1)}, u32[]{:S(2)}, u32[]{:S(2)}) %collective-permute-start.4) | collective-permute-done | bytes 4194336 | tf_op jit(solution)/shard_map/ppermute | solution.py:13
  853.7 4.0 broadcast_select_fusion.4
  862.5 3.0 pad_maximum_fusion.5
  867.4 282.8 %all-reduce.2.cloned.1.call-done = f32[10,256,256]{2,1,0:T(8,128)} async-done(((f32[10,256,256]{2,1,0:T(8,128)}), f32[10,256,256]{2,1,0:T(8,128)}) %all-reduce.2.cloned.1.call-update) | async-done | bytes 2621456 | tf_op jit(solution)/shard_map/psum | solution.py:58
  1151.0 2.0 collective-permute-start.5
  1153.2 12.7 %collective-permute-done.5 = f32[4,16,256]{2,1,0:T(8,128)S(1)} collective-permute-done((f32[4,16,256]{2,1,0:T(8,128)S(1)}, f32[4,16,256]{2,1,0:T(8,128)S(1)}, u32[]{:S(2)}, u32[]{:S(2)}) %collective-permute-start.5) | collective-permute-done | bytes 65568 | tf_op jit(solution)/shard_map/ppermute | solution.py:13
  1167.9 12.1 collective-permute-done.6
  1180.1 1.9 collective-permute-start.7
  1182.1 10.2 collective-permute-done.7
  1194.3 5.4 collective-permute-done.8
  1201.7 5.7 collective-permute-done.9
  (48 shorter events, 21.8 us)
Async XLA Ops:
  6.5 106.8 %copy-start = (bf16[2048,256]{1,0:T(8,128)(2,1)S(1)}, bf16[2048,256]{1,0:T(8,128)(2,1)}, u32[]{:S(2)}) copy-start(bf16[2048,256]{1,0:T(8,128)(2,1)} %param.3) | copy-start | bytes 3145732
  6.5 5.5 copy-start.2
  6.5 1143.7 %all-reduce.2.cloned.1.call-start = ((), (), s32[]{:S(2)}) async-start(), calls=%async_computation | async-start | bytes 5242880 | tf_op jit(solution)/shard_map/psum | solution.py:58
  10.1 103.2 %collective-permute-start = (bf16[4,2048,256]{2,1,0:T(8,128)(2,1)}, bf16[4,2048,256]{2,1,0:T(8,128)(2,1)}, u32[]{:S(2)}, u32[]{:S(2)}) collective-permute-start(bf16[4,2048,256]{2,1,0:T(8,128)(2,1)} %broadcast_in_dim.114), channel_id=1, source_target_pairs={{16,0},{32,16},{48,32},{64,48},{80,64},{96,80},{112,96},{128,112},... | collective-permute-start | bytes 12582920 | tf_op jit(solution)/shard_map/ppermute | solution.py:13
  116.1 182.3 %collective-permute-start.1 = (bf16[4,2048,256]{2,1,0:T(8,128)(2,1)S(1)}, bf16[4,2048,256]{2,1,0:T(8,128)(2,1)S(1)}, u32[]{:S(2)}, u32[]{:S(2)}) collective-permute-start(bf16[4,2048,256]{2,1,0:T(8,128)(2,1)S(1)} %broadcast_select_fusion), channel_id=1, source_target_pairs={{32,0},{48,16},{64,32},{80,48},{96,64},{112,80},{128,96},{144,112}... | collective-permute-start | bytes 12582920 | tf_op jit(solution)/shard_map/ppermute | solution.py:13
  301.1 358.7 %collective-permute-start.2 = (bf16[4,2048,256]{2,1,0:T(8,128)(2,1)S(1)}, bf16[4,2048,256]{2,1,0:T(8,128)(2,1)S(1)}, u32[]{:S(2)}, u32[]{:S(2)}) collective-permute-start(bf16[4,2048,256]{2,1,0:T(8,128)(2,1)S(1)} %broadcast_select_fusion.1), channel_id=1, source_target_pairs={{64,0},{80,16},{96,32},{112,48},{128,64},{144,80},{160,96},{176,11... | collective-permute-start | bytes 12582920 | tf_op jit(solution)/shard_map/ppermute | solution.py:13
  660.3 95.6 %collective-permute-start.3 = (bf16[4,2048,256]{2,1,0:T(8,128)(2,1)S(1)}, bf16[4,2048,256]{2,1,0:T(8,128)(2,1)S(1)}, u32[]{:S(2)}, u32[]{:S(2)}) collective-permute-start(bf16[4,2048,256]{2,1,0:T(8,128)(2,1)S(1)} %broadcast_select_fusion.2), channel_id=1, source_target_pairs={{128,0},{144,16},{160,32},{176,48},{192,64},{208,80},{224,96},{240... | collective-permute-start | bytes 12582920 | tf_op jit(solution)/shard_map/ppermute | solution.py:13
  755.9 4.3 copy-start.1
  758.3 95.4 %collective-permute-start.4 = (bf16[4,2048,256]{2,1,0:T(8,128)(2,1)}, bf16[4,2048,256]{2,1,0:T(8,128)(2,1)}, u32[]{:S(2)}, u32[]{:S(2)}) collective-permute-start(bf16[4,2048,256]{2,1,0:T(8,128)(2,1)} %broadcast_select_fusion.3), channel_id=1, source_target_pairs={{256,0},{272,16},{288,32},{304,48},{320,64},{336,80},{352,96},{368... | collective-permute-start | bytes 12582920 | tf_op jit(solution)/shard_map/ppermute | solution.py:13
  1151.0 14.9 %collective-permute-start.5 = (f32[4,16,256]{2,1,0:T(8,128)S(1)}, f32[4,16,256]{2,1,0:T(8,128)S(1)}, u32[]{:S(2)}, u32[]{:S(2)}) collective-permute-start(f32[4,16,256]{2,1,0:T(8,128)S(1)} %pad_maximum_fusion.10), channel_id=1, source_target_pairs={{16,0},{32,16},{48,32},{64,48},{80,64},{96,80},{112,96},{128,112},... | collective-permute-start | bytes 196616 | tf_op jit(solution)/shard_map/ppermute | solution.py:13
  1166.0 14.1 %collective-permute-start.6 = (f32[4,16,256]{2,1,0:T(8,128)S(1)}, f32[4,16,256]{2,1,0:T(8,128)S(1)}, u32[]{:S(2)}, u32[]{:S(2)}) collective-permute-start(f32[4,16,256]{2,1,0:T(8,128)S(1)} %broadcast_select_fusion.5), channel_id=1, source_target_pairs={{32,0},{48,16},{64,32},{80,48},{96,64},{112,80},{128,96},{144,112}... | collective-permute-start | bytes 196616 | tf_op jit(solution)/shard_map/ppermute | solution.py:13
  1180.1 12.2 %collective-permute-start.7 = (f32[4,16,256]{2,1,0:T(8,128)S(1)}, f32[4,16,256]{2,1,0:T(8,128)S(1)}, u32[]{:S(2)}, u32[]{:S(2)}) collective-permute-start(f32[4,16,256]{2,1,0:T(8,128)S(1)} %broadcast_select_fusion.6), channel_id=1, source_target_pairs={{64,0},{80,16},{96,32},{112,48},{128,64},{144,80},{160,96},{176,11... | collective-permute-start | bytes 196616 | tf_op jit(solution)/shard_map/ppermute | solution.py:13
  1192.4 7.4 collective-permute-start.8
  1199.8 7.7 collective-permute-start.9
Sparse Core Ops, SparseCore 0:
  865.6 284.5 all-reduce.1
where the time goes:
time: 1220 us
  waiting for transfers between devices  1100 us (90%)
  blocking collectives  45.1 us (4%)
  starting transfers between devices  19.3 us (2%)
  other arithmetic  18.6 us (2%)
  between operations  15.4 us (1%)
    ppermute x10, waiting for transfers between devices, shifted_2(): return lax.ppermute(block, axis, route)  821 us
    psum x1, waiting for transfers between devices, per_device(): summed = lax.psum(stacked, 'rep')  283 us
    all_gather x1, blocking collectives, per_device(): lax.all_gather(omega.astype(jnp.bfloat16), 'rep', axis=2, tiled=True)[0]  45.1 us
  transfers between devices with their start and end apart: 11, of which 11 were waited for; matrix products, arithmetic and copies ran while one was open for 0% of the time, Pallas kernels for 0%

commit v1 on v0

--- a/solution.py
+++ b/solution.py
@@ -55,7 +55,8 @@
     left_terms = jnp.einsum("td,ktc->kdc", mixed, gathered, preferred_element_type=jnp.float32)
     stacked = jnp.concatenate([left_terms, jnp.swapaxes(left_terms, 1, 2)], axis=0)
     first_row = replica_index * tile_rows
-    summed = lax.psum(stacked, "rep")
+    shards = lax.all_gather(stacked, "rep", axis=0, tiled=False)
+    summed = shards.sum(axis=0)
     summed = lax.dynamic_slice_in_dim(summed, first_row, tile_rows, 1)
     own_terms = summed[:slot_count]
     flipped = summed[slot_count:]

time: 1220 us -> 1610 us (1.32)
  the two profiles are of different devices: /device:TPU:230 before, /device:TPU:38 now
where the time goes in v1:
time: 1610 us
  waiting for transfers between devices  1360 us (84%)
  starting transfers between devices  139 us (9%)
  blocking collectives  48.3 us (3%)
  other arithmetic  32.7 us (2%)
    ppermute x10, waiting for transfers between devices, shifted_2(): return lax.ppermute(block, axis, route)  728 us
    all_gather x1, waiting for transfers between devices, per_device(): shards = lax.all_gather(stacked, 'rep', axis=0, tiled=False)  631 us
    ppermute x10, starting transfers between devices, shifted_2(): return lax.ppermute(block, axis, route)  139 us
    all_gather x1, blocking collectives, per_device(): lax.all_gather(omega.astype(jnp.bfloat16), 'rep', axis=2, tiled=True)[0]  48.3 us
  transfers between devices with their start and end apart: 11, of which 11 were waited for; matrix products, arithmetic and copies ran while one was open for 0% of the time, Pallas kernels for 0%

profile of v1, /device:TPU:38, one launch (start us, length us, event | category | flops | bytes accessed | tf_op | source)
XLA Modules:
  0.0 1607.3 jit_solution(8769989886391807747)
XLA Ops:
  6.5 3.5 broadcast_in_dim.114
  16.8 87.9 %collective-permute-done = bf16[4,2048,256]{2,1,0:T(8,128)(2,1)} collective-permute-done((bf16[4,2048,256]{2,1,0:T(8,128)(2,1)}, bf16[4,2048,256]{2,1,0:T(8,128)(2,1)}, u32[]{:S(2)}, u32[]{:S(2)}) %collective-permute-start) | collective-permute-done | bytes 4194336 | tf_op jit(solution)/shard_map/ppermute | solution.py:13
  104.8 2.7 broadcast_select_fusion
  107.4 19.4 %collective-permute-start.1 = (bf16[4,2048,256]{2,1,0:T(8,128)(2,1)S(1)}, bf16[4,2048,256]{2,1,0:T(8,128)(2,1)S(1)}, u32[]{:S(2)}, u32[]{:S(2)}) collective-permute-start(bf16[4,2048,256]{2,1,0:T(8,128)(2,1)S(1)} %broadcast_select_fusion), channel_id=1, source_target_pairs={{32,0},{48,16},{64,32},{80,48},{96,64},{112,80},{128,96},{144,112}... | collective-permute-start | bytes 12582920 | tf_op jit(solution)/shard_map/ppermute | solution.py:13
  126.8 171.3 %collective-permute-done.1 = bf16[4,2048,256]{2,1,0:T(8,128)(2,1)S(1)} collective-permute-done((bf16[4,2048,256]{2,1,0:T(8,128)(2,1)S(1)}, bf16[4,2048,256]{2,1,0:T(8,128)(2,1)S(1)}, u32[]{:S(2)}, u32[]{:S(2)}) %collective-permute-start.1) | collective-permute-done | bytes 4194336 | tf_op jit(solution)/shard_map/ppermute | solution.py:13
  298.1 2.9 broadcast_select_fusion.1
  302.9 271.9 %collective-permute-done.2 = bf16[4,2048,256]{2,1,0:T(8,128)(2,1)S(1)} collective-permute-done((bf16[4,2048,256]{2,1,0:T(8,128)(2,1)S(1)}, bf16[4,2048,256]{2,1,0:T(8,128)(2,1)S(1)}, u32[]{:S(2)}, u32[]{:S(2)}) %collective-permute-start.2) | collective-permute-done | bytes 4194336 | tf_op jit(solution)/shard_map/ppermute | solution.py:13
  575.3 2.5 collective-permute-start.3
  577.8 93.0 %collective-permute-done.3 = bf16[4,2048,256]{2,1,0:T(8,128)(2,1)S(1)} collective-permute-done((bf16[4,2048,256]{2,1,0:T(8,128)(2,1)S(1)}, bf16[4,2048,256]{2,1,0:T(8,128)(2,1)S(1)}, u32[]{:S(2)}, u32[]{:S(2)}) %collective-permute-start.3) | collective-permute-done | bytes 4194336 | tf_op jit(solution)/shard_map/ppermute | solution.py:13
  670.8 2.4 broadcast_select_fusion.3
  675.4 48.3 %all_gather.9 = bf16[1,5,256,256]{3,2,1,0:T(8,128)(2,1)S(1)} all-gather(bf16[1,5,16,256]{3,2,1,0:T(8,128)(2,1)S(1)} %convert_element_type.6), channel_id=1, replica_groups=mesh['blk'=32,'rep'=16] {'rep'}, dimensions={2}, use_global_device_ids=true | all-gather | bytes 696320 | tf_op jit(solution)/shard_map/all_gather | solution.py:45
  724.3 44.2 %collective-permute-done.4 = bf16[4,2048,256]{2,1,0:T(8,128)(2,1)} collective-permute-done((bf16[4,2048,256]{2,1,0:T(8,128)(2,1)}, bf16[4,2048,256]{2,1,0:T(8,128)(2,1)}, u32[]{:S(2)}, u32[]{:S(2)}) %collective-permute-start.4) | collective-permute-done | bytes 4194336 | tf_op jit(solution)/shard_map/ppermute | solution.py:13
  768.6 4.0 broadcast_select_fusion.4
  777.3 3.1 pad_maximum_fusion.5
  782.4 630.9 %all-gather.3.cloned.1.call-done = f32[160,256,256]{2,1,0:T(8,128)} async-done(((f32[10,256,256]{2,1,0:T(8,128)}), f32[160,256,256]{2,1,0:T(8,128)}) %all-gather.3.cloned.1.call-update) | async-done | bytes 41943056 | tf_op jit(solution)/shard_map/all_gather | solution.py:58
  1413.3 14.8 reduce_sum.18
  1428.2 100.6 %collective-permute-start.5 = (f32[4,16,256]{2,1,0:T(8,128)S(1)}, f32[4,16,256]{2,1,0:T(8,128)S(1)}, u32[]{:S(2)}, u32[]{:S(2)}) collective-permute-start(f32[4,16,256]{2,1,0:T(8,128)S(1)} %pad_maximum_fusion.10), channel_id=1, source_target_pairs={{16,0},{32,16},{48,32},{64,48},{80,64},{96,80},{112,96},{128,112},... | collective-permute-start | bytes 196616 | tf_op jit(solution)/shard_map/ppermute | solution.py:13
  1529.0 15.1 collective-permute-done.5
  1546.1 25.7 %collective-permute-done.6 = f32[4,16,256]{2,1,0:T(8,128)S(1)} collective-permute-done((f32[4,16,256]{2,1,0:T(8,128)S(1)}, f32[4,16,256]{2,1,0:T(8,128)S(1)}, u32[]{:S(2)}, u32[]{:S(2)}) %collective-permute-start.6) | collective-permute-done | bytes 65568 | tf_op jit(solution)/shard_map/ppermute | solution.py:13
  1571.9 4.0 collective-permute-start.7
  1575.9 7.3 collective-permute-done.7
  1583.3 2.5 collective-permute-start.8
  1585.8 5.6 collective-permute-done.8
  1593.3 5.7 collective-permute-done.9
  (49 shorter events, 22.5 us)
Async XLA Ops:
  6.5 98.2 %copy-start = (bf16[2048,256]{1,0:T(8,128)(2,1)S(1)}, bf16[2048,256]{1,0:T(8,128)(2,1)}, u32[]{:S(2)}) copy-start(bf16[2048,256]{1,0:T(8,128)(2,1)} %param.3) | copy-start | bytes 3145732
  6.5 5.5 copy-start.2
  6.5 1406.8 %all-gather.3.cloned.1.call-start = ((), (), s32[]{:S(2)}) async-start(), calls=%async_computation | async-start | bytes 44564480 | tf_op jit(solution)/shard_map/all_gather | solution.py:58
  10.1 94.7 %collective-permute-start = (bf16[4,2048,256]{2,1,0:T(8,128)(2,1)}, bf16[4,2048,256]{2,1,0:T(8,128)(2,1)}, u32[]{:S(2)}, u32[]{:S(2)}) collective-permute-start(bf16[4,2048,256]{2,1,0:T(8,128)(2,1)} %broadcast_in_dim.114), channel_id=1, source_target_pairs={{16,0},{32,16},{48,32},{64,48},{80,64},{96,80},{112,96},{128,112},... | collective-permute-start | bytes 12582920 | tf_op jit(solution)/shard_map/ppermute | solution.py:13
  107.4 190.7 %collective-permute-start.1 = (bf16[4,2048,256]{2,1,0:T(8,128)(2,1)S(1)}, bf16[4,2048,256]{2,1,0:T(8,128)(2,1)S(1)}, u32[]{:S(2)}, u32[]{:S(2)}) collective-permute-start(bf16[4,2048,256]{2,1,0:T(8,128)(2,1)S(1)} %broadcast_select_fusion), channel_id=1, source_target_pairs={{32,0},{48,16},{64,32},{80,48},{96,64},{112,80},{128,96},{144,112}... | collective-permute-start | bytes 12582920 | tf_op jit(solution)/shard_map/ppermute | solution.py:13
  301.0 273.8 %collective-permute-start.2 = (bf16[4,2048,256]{2,1,0:T(8,128)(2,1)S(1)}, bf16[4,2048,256]{2,1,0:T(8,128)(2,1)S(1)}, u32[]{:S(2)}, u32[]{:S(2)}) collective-permute-start(bf16[4,2048,256]{2,1,0:T(8,128)(2,1)S(1)} %broadcast_select_fusion.1), channel_id=1, source_target_pairs={{64,0},{80,16},{96,32},{112,48},{128,64},{144,80},{160,96},{176,11... | collective-permute-start | bytes 12582920 | tf_op jit(solution)/shard_map/ppermute | solution.py:13
  575.3 95.5 %collective-permute-start.3 = (bf16[4,2048,256]{2,1,0:T(8,128)(2,1)S(1)}, bf16[4,2048,256]{2,1,0:T(8,128)(2,1)S(1)}, u32[]{:S(2)}, u32[]{:S(2)}) collective-permute-start(bf16[4,2048,256]{2,1,0:T(8,128)(2,1)S(1)} %broadcast_select_fusion.2), channel_id=1, source_target_pairs={{128,0},{144,16},{160,32},{176,48},{192,64},{208,80},{224,96},{240... | collective-permute-start | bytes 12582920 | tf_op jit(solution)/shard_map/ppermute | solution.py:13
  670.8 4.5 copy-start.1
  673.3 95.3 %collective-permute-start.4 = (bf16[4,2048,256]{2,1,0:T(8,128)(2,1)}, bf16[4,2048,256]{2,1,0:T(8,128)(2,1)}, u32[]{:S(2)}, u32[]{:S(2)}) collective-permute-start(bf16[4,2048,256]{2,1,0:T(8,128)(2,1)} %broadcast_select_fusion.3), channel_id=1, source_target_pairs={{256,0},{272,16},{288,32},{304,48},{320,64},{336,80},{352,96},{368... | collective-permute-start | bytes 12582920 | tf_op jit(solution)/shard_map/ppermute | solution.py:13
  1428.2 115.9 %collective-permute-start.5 = (f32[4,16,256]{2,1,0:T(8,128)S(1)}, f32[4,16,256]{2,1,0:T(8,128)S(1)}, u32[]{:S(2)}, u32[]{:S(2)}) collective-permute-start(f32[4,16,256]{2,1,0:T(8,128)S(1)} %pad_maximum_fusion.10), channel_id=1, source_target_pairs={{16,0},{32,16},{48,32},{64,48},{80,64},{96,80},{112,96},{128,112},... | collective-permute-start | bytes 196616 | tf_op jit(solution)/shard_map/ppermute | solution.py:13
  1544.2 27.7 %collective-permute-start.6 = (f32[4,16,256]{2,1,0:T(8,128)S(1)}, f32[4,16,256]{2,1,0:T(8,128)S(1)}, u32[]{:S(2)}, u32[]{:S(2)}) collective-permute-start(f32[4,16,256]{2,1,0:T(8,128)S(1)} %broadcast_select_fusion.5), channel_id=1, source_target_pairs={{32,0},{48,16},{64,32},{80,48},{96,64},{112,80},{128,96},{144,112}... | collective-permute-start | bytes 196616 | tf_op jit(solution)/shard_map/ppermute | solution.py:13
  1571.9 11.3 collective-permute-start.7
  1583.3 8.1 collective-permute-start.8
  1591.4 7.7 collective-permute-start.9
Sparse Core Ops, SparseCore 0:
  780.5 632.7 all-gather.2
